TPU v7x, 512 devices: a whole 4x4x16 slice. The times are simulated.
512 devices in a mesh: dp: 32 (over x_lo, z), seq: 4 (over y), mp: 4 (over x_hi, core).
Axes of the slice: x: 4 (x_hi: 2, x_lo: 2; x = x_hi * 2 + x_lo), y: 4, z: 16, core: 2. Of those that a mesh axis runs over, the one named last changes fastest.
Arguments:
- hidden: bfloat16 [32768, 6656], P(('dp', 'seq'), 'mp'), may hold values from -6 to 6
- cotangent: bfloat16 [32768, 17920], P(('dp', 'seq'), 'mp'), may hold values from -6 to 6
- frozen_down: bfloat16 [6656, 4], P('mp'), may hold values from -0.078125 to 0.078125
- adapter: float32 [4, 4, 4480], P('mp', None, ('dp', 'seq')), may hold values from -6 to 6
- prior: float32 [48], replicated, may hold values from 0.2 to 5
- domain_of: int32 [64], P('dp'), may hold values from 0 to 47
Outputs:
- new_adapter: float32 [4, 4, 4480], P('mp', None, ('dp', 'seq'))
- log_weights: float32 [48], replicated
All inputs are finite; a program needn't handle non-finite values.
Results may differ from a plain program's by a relative error of at most 0.014.
Values may be sent and summed in bfloat16 or wider, within the bound.
A program may use at most 64 MiB of HBM per device.

v0:
```python
import jax
import jax.numpy as jnp
from jax import lax
from jax.sharding import PartitionSpec as P

FF = 17920
NDOM = 48
RANK = 4
step_rate = 1.0
learn_rate = 0.5


def expand_weights(weights):
    return (weights[:, None, None] * jnp.eye(RANK, dtype=jnp.float32)[None, :, :]).reshape(
        NDOM * RANK, RANK
    )


def domain_scores(terms, mixture):
    return jnp.sum(terms.reshape(terms.shape[0], NDOM, RANK) * mixture[:, None, :], axis=(0, 2))


def reweight(weights, scores, sumsq):
    meansq = sumsq / (RANK * FF) + 1e-06
    ratio = scores / (RANK * FF * meansq)
    raised = weights * jnp.exp(step_rate * ratio)
    log_new = jnp.log(weights) + step_rate * ratio - jnp.log(jnp.sum(raised))
    return (log_new, meansq)


def body(hidden, cotangent, frozen_down, adapter, prior, domain_of):
    rows = hidden.shape[0]
    piece = rows // domain_of.shape[0]
    partial_down = jnp.dot(hidden, frozen_down, preferred_element_type=jnp.float32)
    down = lax.psum(partial_down.astype(jnp.bfloat16), "mp")
    domain_tok = jnp.repeat(domain_of, piece, total_repeat_length=rows)
    onehot = (domain_tok[:, None] == jnp.arange(NDOM, dtype=jnp.int32)[None, :]).astype(
        jnp.bfloat16
    )
    spread = (onehot[:, :, None] * down[:, None, :]).reshape(rows, NDOM * RANK)
    weights = prior / jnp.sum(prior)
    highest = lax.Precision.HIGHEST
    shard = lax.psum_scatter(
        lax.dot_general(
            cotangent, spread, (((0,), (0,)), ((), ())), preferred_element_type=jnp.float32
        ),
        ("dp", "seq"),
        scatter_dimension=0,
        tiled=True,
    )
    mixture = jnp.dot(shard, expand_weights(weights), precision=highest)
    scores, sumsq = lax.psum(
        (domain_scores(shard, mixture), jnp.sum(mixture * mixture)), ("dp", "seq", "mp")
    )
    log_new, meansq = reweight(weights, scores, sumsq)
    update = jnp.dot(shard, expand_weights(jnp.exp(log_new)), precision=highest)
    new_adapter = adapter - learn_rate * update.T[None, :, :] / jnp.sqrt(meansq)
    return (new_adapter, log_new)


def solution(mesh):
    return jax.shard_map(
        body,
        mesh=mesh,
        in_specs=(
            P(("dp", "seq"), "mp"),
            P(("dp", "seq"), "mp"),
            P("mp", None),
            P("mp", None, ("dp", "seq")),
            P(),
            P("dp"),
        ),
        out_specs=(P("mp", None, ("dp", "seq")), P()),
        check_vma=False,
    )
```

profile of v0, /device:TPU:1, one launch (start us, length us, event | category | flops | bytes accessed | tf_op | source)
XLA Modules:
  0.0 1317.5 jit_solution(4457269442039612143)
XLA Ops:
  7.2 0.0 all-reduce.4.cloned.1.call-start
  7.2 1.4 fusion.17
  8.7 1.3 compare_select_fusion.1
  10.0 1.4 convolution_convert_fusion
  11.4 13.4 %psum.21 = bf16[256,4]{0,1:T(4,128)(2,1)S(1)} all-reduce(bf16[256,4]{0,1:T(4,128)(2,1)S(1)} %convolution_convert_fusion), channel_id=1, replica_groups=mesh['dp'=32,'seq'=4,'mp'=4] {'mp'}, use_global_device_ids=true, to_apply=%region_1.2 | all-reduce | flops 1024 | bytes 4096 | tf_op jit(solution)/shard_map/psum | solution.py:35
  24.9 0.1 broadcast_multiply_fusion
  25.0 2.4 convolution_bitcast_fusion
  27.4 0.6 copy-done.2
  28.0 0.6 reduce_sum.43
  28.6 0.6 broadcast_divide_fusion.1
  29.3 0.1 mul.88
  29.4 0.1 mul.89
  29.5 1.3 dynamic-slice.6
  31.4 1092.8 %all-reduce.4.cloned.1.call-done = f32[4480,192]{0,1:T(8,128)} async-done(((f32[4480,192]{0,1:T(8,128)}), f32[4480,192]{0,1:T(8,128)}) %all-reduce.4.cloned.1.call-update) | async-done | bytes 3440656
  1124.3 1.9 multiply_reduce_fusion.1
  1126.2 1.1 multiply_reduce_fusion
  1127.3 0.1 reduce_sum.45
  1127.5 0.1 reduce_sum.46
  1127.6 177.2 %all-reduce.1 = (f32[48]{0:T(128)S(1)}, f32[]{:T(128)}) all-reduce(f32[48]{0:T(128)S(1)} %reduce_sum.46, f32[]{:T(128)} %get-tuple-element.22), channel_id=1, replica_groups=mesh['dp'=32,'seq'=4,'mp'=4] {'dp','seq','mp'}, use_global_device_ids=true, to_apply=%region_5.6 | all-reduce | flops 49 | bytes 392 | tf_op jit(solution)/shard_map/psum | solution.py:52
  1305.4 1.3 multiply_reduce_fusion.2
  1307.4 1.2 fusion.16
  1308.6 0.1 mul.100
  1308.6 0.1 mul.101
  1308.8 1.9 fusion.2
  (14 shorter events, 0.1 us)
Async XLA Ops:
  7.2 17.8 %copy-start = (bf16[256,4480]{1,0:T(8,128)(2,1)S(1)}, bf16[256,4480]{1,0:T(8,128)(2,1)}, u32[]{:S(2)}) copy-start(bf16[256,4480]{1,0:T(8,128)(2,1)} %param.9) | copy-start | bytes 6881284
  7.2 1117.1 %all-reduce.4.cloned.1.call-start = ((), (), s32[]{:S(2)}) async-start(), calls=%async_computation | async-start | bytes 6881280
  27.4 0.7 copy-start.2
  27.4 1281.4 %copy-start.1 = (f32[1,4,35]{2,1,0:T(4,128)S(1)}, f32[1,4,35]{2,1,0:T(4,128)}, u32[]{:S(2)}) copy-start(f32[1,4,35]{2,1,0:T(4,128)} %param.11) | copy-start | bytes 1684
Sparse Core Ops, SparseCore 0:
  27.5 1096.6 all-reduce.3
where the time goes:
time: 1320 us
  waiting for transfers between devices  1090 us (83%)
  blocking collectives  191 us (14%)
  between operations  16.2 us (1%)
    unnamed x2, waiting for transfers between devices  1090 us
    psum x1, blocking collectives, body(): lax.psum((domain_scores(shard, mixture), jnp.sum(mixture * mixture)), ('d...  177 us
  transfers between devices with their start and end apart: 1, of which 1 were waited for; matrix products, arithmetic and copies ran while one was open for 0% of the time, Pallas kernels for 0%

commit v1 on v0

--- a/solution.py
+++ b/solution.py
@@ -50,7 +50,7 @@
     )
     mixture = jnp.dot(shard, expand_weights(weights), precision=highest)
     scores, sumsq = lax.psum(
-        (domain_scores(shard, mixture), jnp.sum(mixture * mixture)), ("dp", "seq", "mp")
+        lax.psum((domain_scores(shard, mixture), jnp.sum(mixture * mixture)), "dp"), ("seq", "mp")
     )
     log_new, meansq = reweight(weights, scores, sumsq)
     update = jnp.dot(shard, expand_weights(jnp.exp(log_new)), precision=highest)

time: 1320 us -> 1310 us (level)
    psum x1 -> x2, blocking collectives: 177 us -> 170 us  [the longest x1 121 us: body(): lax.psum(lax.psum((domain_scores(shard, mixture), jnp.sum(mixture * mixtu...]
where the time goes in v1:
time: 1310 us
  waiting for transfers between devices  1090 us (83%)
  blocking collectives  184 us (14%)
  between operations  16.2 us (1%)
    unnamed x2, waiting for transfers between devices  1090 us
    psum x1, blocking collectives, body(): lax.psum(lax.psum((domain_scores(shard, mixture), jnp.sum(mixture * mixtu...  121 us
    psum x1, blocking collectives, body(): lax.psum((domain_scores(shard, mixture), jnp.sum(mixture * mixture)), 'dp')  49.4 us
  transfers between devices with their start and end apart: 1, of which 1 were waited for; matrix products, arithmetic and copies ran while one was open for 0% of the time, Pallas kernels for 0%

profile of v1, /device:TPU:1, one launch (start us, length us, event | category | flops | bytes accessed | tf_op | source)
XLA Modules:
  0.0 1310.6 jit_solution(15635422688329075307)
XLA Ops:
  7.2 1.4 fusion.17
  8.7 1.3 compare_select_fusion.1
  10.0 1.4 convolution_convert_fusion
  11.4 13.4 %psum.35 = bf16[256,4]{0,1:T(4,128)(2,1)S(1)} all-reduce(bf16[256,4]{0,1:T(4,128)(2,1)S(1)} %convolution_convert_fusion), channel_id=1, replica_groups=mesh['dp'=32,'seq'=4,'mp'=4] {'mp'}, use_global_device_ids=true, to_apply=%region_1.2 | all-reduce | flops 1024 | bytes 4096 | tf_op jit(solution)/shard_map/psum | solution.py:35
  24.9 0.1 broadcast_multiply_fusion
  25.0 2.4 convolution_bitcast_fusion
  27.4 0.6 copy-done.2
  28.0 0.6 reduce_sum.43
  28.6 0.6 broadcast_divide_fusion.1
  29.3 0.1 mul.88
  29.4 0.1 mul.89
  29.5 1.3 dynamic-slice.6
  31.4 1092.8 %all-reduce.5.cloned.1.call-done = f32[4480,192]{0,1:T(8,128)} async-done(((f32[4480,192]{0,1:T(8,128)}), f32[4480,192]{0,1:T(8,128)}) %all-reduce.5.cloned.1.call-update) | async-done | bytes 3440656
  1124.3 1.9 multiply_reduce_fusion.1
  1126.2 1.1 multiply_reduce_fusion
  1127.3 0.1 reduce_sum.45
  1127.5 0.1 reduce_sum.46
  1127.6 49.4 %all-reduce.1 = (f32[48]{0:T(128)S(1)}, f32[]{:T(128)}) all-reduce(f32[48]{0:T(128)S(1)} %reduce_sum.46, f32[]{:T(128)} %get-tuple-element.24), channel_id=1, replica_groups=mesh['dp'=32,'seq'=4,'mp'=4] {'dp'}, use_global_device_ids=true, to_apply=%region_5.6 | all-reduce | flops 49 | bytes 392 | tf_op jit(solution)/shard_map/psum | solution.py:53
  1177.0 120.9 %all-reduce.2 = (f32[48]{0:T(128)S(1)}, f32[]{:T(128)}) all-reduce(f32[48]{0:T(128)S(1)} %get-tuple-element.14, f32[]{:T(128)} %get-tuple-element.15), channel_id=1, replica_groups=mesh['dp'=32,'seq'=4,'mp'=4] {'seq','mp'}, use_global_device_ids=true, to_apply=%region_6.7 | all-reduce | flops 49 | bytes 392 | tf_op jit(solution)/shard_map/psum | solution.py:52
  1298.6 1.3 multiply_reduce_fusion.2
  1300.5 1.2 fusion.16
  1301.7 0.1 mul.100
  1301.8 0.1 mul.101
  1301.9 1.9 fusion.2
  (15 shorter events, 0.2 us)
Async XLA Ops:
  7.2 17.8 %copy-start = (bf16[256,4480]{1,0:T(8,128)(2,1)S(1)}, bf16[256,4480]{1,0:T(8,128)(2,1)}, u32[]{:S(2)}) copy-start(bf16[256,4480]{1,0:T(8,128)(2,1)} %param.9) | copy-start | bytes 6881284
  7.2 1117.1 %all-reduce.5.cloned.1.call-start = ((), (), s32[]{:S(2)}) async-start(), calls=%async_computation | async-start | bytes 6881280
  27.4 0.7 copy-start.2
  27.4 1274.5 %copy-start.1 = (f32[1,4,35]{2,1,0:T(4,128)S(1)}, f32[1,4,35]{2,1,0:T(4,128)}, u32[]{:S(2)}) copy-start(f32[1,4,35]{2,1,0:T(4,128)} %param.11) | copy-start | bytes 1684
Sparse Core Ops, SparseCore 0:
  27.5 1096.6 all-reduce.4
